TPU v7x, 32 devices: a whole 2x2x4 slice. The times are simulated.
32 devices in a mesh: dp: 4 (over y, x), mp: 8 (over z, core).
Axes of the slice: x: 2, y: 2, z: 4, core: 2. Of those that a mesh axis runs over, the one named last changes fastest.
Arguments:
- tokens: bfloat16 [512, 6144], P(('dp', 'mp')), may hold values from -6 to 6
- norm_gain: float32 [6144], replicated, may hold values from 0.5 to 1.5
- up_weight: bfloat16 [6144, 16384], P(None, 'mp'), may hold values from -0.078125 to 0.078125
- down_weight: bfloat16 [16384, 6144], P('mp'), may hold values from -0.046875 to 0.046875
- out_grad: bfloat16 [512, 6144], P(('dp', 'mp')), may hold values from -6 to 6
Outputs:
- input_grad: bfloat16 [512, 6144], P(('dp', 'mp'))
- up_grad: bfloat16 [6144, 16384], P('dp', 'mp')
- down_grad: bfloat16 [16384, 6144], P('mp', 'dp')
- gain_grad: float32 [6144], replicated
All inputs are finite; a program needn't handle non-finite values.
Results may differ from a plain program's by a relative error of at most 0.018.
Values may be sent and summed in bfloat16 or wider, within the bound.
No kernel may reach another device: no remote copies, remote signals or barrier semaphores. Data moves between devices by JAX's collectives and lax.ppermute only.
A program may use at most 192 MiB of HBM per device.

v0:
```python
import math
import jax
import jax.numpy as jnp
from jax import lax
from jax.sharding import PartitionSpec as P


def gelu_value(preact):
    return 0.5 * preact * (1.0 + lax.erf(preact * 0.7071067811865476))


def gelu_slope(preact):
    return (
        0.5 * (1.0 + lax.erf(preact * 0.7071067811865476))
        + preact * jnp.exp(-0.5 * preact * preact) * 0.3989422804014327
    )


def per_device(tokens, norm_gain, up_weight, down_weight, out_grad):
    values = tokens.astype(jnp.float32)
    centered = values - jnp.mean(values, axis=1, keepdims=True)
    inv_std = lax.rsqrt(jnp.mean(centered * centered, axis=1, keepdims=True) + 1e-06)
    x_hat = centered * inv_std
    normed = (x_hat * norm_gain).astype(jnp.bfloat16)
    normed_all, cotan_all = (
        lax.all_gather(normed, "mp", axis=0, tiled=True),
        lax.all_gather(out_grad, "mp", axis=0, tiled=True),
    )
    preact = jnp.dot(normed_all, up_weight, preferred_element_type=jnp.float32)
    hidden = gelu_value(preact).astype(jnp.bfloat16)
    hid_grad = lax.dot_general(
        cotan_all, down_weight, (((1,), (1,)), ((), ())), preferred_element_type=jnp.float32
    )
    pre_grad = (hid_grad * gelu_slope(preact)).astype(jnp.bfloat16)
    norm_grad = lax.psum_scatter(
        lax.dot_general(
            pre_grad, up_weight, (((1,), (1,)), ((), ())), preferred_element_type=jnp.float32
        ),
        "mp",
        scatter_dimension=0,
        tiled=True,
    )
    replicas = lax.axis_size("dp")
    group = normed_all.shape[0]
    factor = 1.0 / math.sqrt(group * replicas)
    gain_grad = lax.psum(jnp.sum(norm_grad * x_hat, axis=0), ("dp", "mp")) * factor
    scaled = norm_gain * norm_grad
    input_grad = (
        scaled
        - jnp.mean(scaled, axis=1, keepdims=True)
        - x_hat * jnp.mean(scaled * x_hat, axis=1, keepdims=True)
    ) * inv_std
    normed_cols, cotan_cols = (
        lax.all_to_all(normed_all, "dp", split_axis=1, concat_axis=0, tiled=True),
        lax.all_to_all(cotan_all, "dp", split_axis=1, concat_axis=0, tiled=True),
    )
    hidden_all, pre_all = (
        lax.all_gather(hidden, "dp", axis=0, tiled=True),
        lax.all_gather(pre_grad, "dp", axis=0, tiled=True),
    )

    def stacked(array):
        return array.reshape(replicas, group, array.shape[1])

    up_parts = jnp.einsum(
        "rtk,rtf->rkf", stacked(normed_cols), stacked(pre_all), preferred_element_type=jnp.float32
    )
    down_parts = jnp.einsum(
        "rtf,rtk->rfk", stacked(hidden_all), stacked(cotan_cols), preferred_element_type=jnp.float32
    )
    up_total = jnp.sum(up_parts.astype(jnp.bfloat16).astype(jnp.float32), axis=0)
    down_total = jnp.sum(down_parts.astype(jnp.bfloat16).astype(jnp.float32), axis=0)
    up_grad = (up_total * factor).astype(jnp.bfloat16)
    down_grad = (down_total * factor).astype(jnp.bfloat16)
    return (input_grad.astype(jnp.bfloat16), up_grad, down_grad, gain_grad)


def solution(mesh):
    placed = (P(("dp", "mp"), None), P(), P(None, "mp"), P("mp", None), P(("dp", "mp"), None))
    return jax.shard_map(
        per_device,
        mesh=mesh,
        in_specs=placed,
        out_specs=(P(("dp", "mp"), None), P("dp", "mp"), P("mp", "dp"), P()),
        check_vma=False,
    )
```

profile of v0, /device:TPU:10, one launch (start us, length us, event | category | flops | bytes accessed | tf_op | source)
XLA Modules:
  0.0 251.2 jit_solution(14012743861452806159)
XLA Ops:
  7.2 0.0 all-gather.7.cloned.1.call-start
  7.2 1.1 convert_reduce_fusion.2
  8.3 1.2 fusion.19
  9.5 1.7 fusion.13
  11.2 0.0 all-gather.7.cloned.1.call-update
  11.2 0.0 all-gather.5.cloned.1.call-start
  11.3 0.7 all-gather.5.cloned.1.call-update
  12.0 0.0 all-gather.11.cloned.1.call-start
  12.0 25.4 %all-gather.7.cloned.1.call-done = bf16[128,6144]{1,0:T(8,128)(2,1)} async-done(((bf16[16,6144]{1,0:T(8,128)(2,1)}), bf16[128,6144]{1,0:T(8,128)(2,1)}) %all-gather.7.cloned.1.call-update) | async-done | bytes 1572880 | tf_op jit(solution)/shard_map/all_gather | solution.py:26
  37.5 13.1 %multiply_convert_fusion.2 = (bf16[128,2048]{1,0:T(8,128)(2,1)}, f32[128,2048]{1,0:T(8,128)S(1)}) fusion(bf16[128,6144]{1,0:T(8,128)(2,1)} %all-gather.7.cloned.1.call-done, bf16[6144,2048]{1,0:T(8,128)(2,1)} %param.7), kind=kOutput, calls=%fused_computation.15 | convolution fusion | flops 3222536192 | bytes 28311552 | tf_op jit(solution)/shard_map/dot_general | solution.py:29
  50.6 0.0 all-gather.11.cloned.1.call-update
  50.6 0.0 all-gather.9.cloned.1.call-start
  50.6 12.9 %all-gather.5.cloned.1.call-done = bf16[128,6144]{1,0:T(8,128)(2,1)} async-done(((bf16[16,6144]{1,0:T(8,128)(2,1)}), bf16[128,6144]{1,0:T(8,128)(2,1)}) %all-gather.5.cloned.1.call-update) | async-done | bytes 1572880 | tf_op jit(solution)/shard_map/all_gather | solution.py:27
  63.5 14.3 %fusion = bf16[128,2048]{1,0:T(8,128)(2,1)} fusion(bf16[128,6144]{1,0:T(8,128)(2,1)} %all-gather.5.cloned.1.call-done, bf16[2048,6144]{1,0:T(8,128)(2,1)} %param.8, f32[128,2048]{1,0:T(8,128)S(1)} %get-tuple-element.8), kind=kOutput, calls=%fused_computation.7 | convolution fusion | flops 3223846912 | bytes 28311552 | tf_op jit(solution)/shard_map/dot_general | solution.py:31
  77.8 0.0 all-gather.9.cloned.1.call-update
  77.8 0.0 copy-start
  77.9 0.0 reduce-scatter.2.cloned.1.call-start
  77.9 14.4 %fusion.20 = f32[128,6144]{1,0:T(8,128)} fusion(bf16[128,2048]{1,0:T(8,128)(2,1)} %fusion, bf16[6144,2048]{1,0:T(8,128)(2,1)} %param.7), kind=kOutput, calls=%fused_computation.38 | convolution fusion | flops 3221225472 | bytes 28835840 | tf_op jit(solution)/shard_map/dot_general | solution.py:36
  92.4 0.0 copy-start.1
  92.4 0.0 reduce-scatter.2.cloned.1.call-update
  92.4 0.0 copy-done
  92.4 1.6 copy.16
  94.0 2.6 %copy.17 = bf16[128,4,1536]{2,0,1:T(8,128)(2,1)} copy(bf16[128,4,1536]{0,2,1:T(8,128)(2,1)} %bitcast.18) | data formatting | bytes 3145728 | tf_op jit(solution)/shard_map/all_to_all | solution.py:55
  96.5 4.2 %all-to-all-start.1 = ((bf16[128,4,1536]{2,0,1:T(8,128)(2,1)}), bf16[128,4,1536]{2,0,1:T(8,128)(2,1)S(1)}, u32[]{:S(2)}, u32[]{:S(2)}) async-start(bf16[128,4,1536]{2,0,1:T(8,128)(2,1)} %copy.17), calls=%async_computation.2 | async-start | bytes 3145728 | tf_op jit(solution)/shard_map/all_to_all | solution.py:55
  100.7 0.0 copy-done.1
  100.7 1.6 copy.20
  102.3 23.3 %all-to-all-done.1 = bf16[128,4,1536]{2,0,1:T(8,128)(2,1)S(1)} async-done(((bf16[128,4,1536]{2,0,1:T(8,128)(2,1)}), bf16[128,4,1536]{2,0,1:T(8,128)(2,1)S(1)}, u32[]{:S(2)}, u32[]{:S(2)}) %all-to-all-start.1) | async-done | bytes 1572896 | tf_op jit(solution)/shard_map/all_to_all | solution.py:55
  125.6 4.1 %all-to-all-start = ((bf16[128,4,1536]{0,2,1:T(8,128)(2,1)}), bf16[128,4,1536]{0,2,1:T(8,128)(2,1)S(1)}, u32[]{:S(2)}, u32[]{:S(2)}) async-start(bf16[128,4,1536]{0,2,1:T(8,128)(2,1)} %bitcast), calls=%async_computation.1 | async-start | bytes 3145728 | tf_op jit(solution)/shard_map/all_to_all | solution.py:54
  129.7 0.0 all-gather.11.cloned.1.call-done
  129.7 14.2 %convert_reduce_fusion = f32[2048,1536]{1,0:T(8,128)} fusion(bf16[4,128,2048]{2,1,0:T(8,128)(2,1)} %bitcast.19, bf16[128,4,1536]{2,0,1:T(8,128)(2,1)S(1)} %all-to-all-done.1), kind=kOutput, calls=%fused_computation | convolution fusion | flops 3255828480 | bytes 16252928 | tf_op jit(solution)/shard_map/rtf,rtk->rfk/dot_general | solution.py:68
  143.9 15.4 %all-to-all-done = bf16[128,4,1536]{0,2,1:T(8,128)(2,1)S(1)} async-done(((bf16[128,4,1536]{0,2,1:T(8,128)(2,1)}), bf16[128,4,1536]{0,2,1:T(8,128)(2,1)S(1)}, u32[]{:S(2)}, u32[]{:S(2)}) %all-to-all-start) | async-done | bytes 1572896 | tf_op jit(solution)/shard_map/all_to_all | solution.py:54
  159.3 0.0 all-gather.9.cloned.1.call-done
  159.3 14.0 %convert_reduce_fusion.1 = f32[1536,2048]{1,0:T(8,128)} fusion(bf16[4,128,2048]{2,1,0:T(8,128)(2,1)} %bitcast.20, bf16[128,4,1536]{0,2,1:T(8,128)(2,1)S(1)} %all-to-all-done), kind=kOutput, calls=%fused_computation.1 | convolution fusion | flops 3255828480 | bytes 16252928 | tf_op jit(solution)/shard_map/rtk,rtf->rkf/dot_general | solution.py:65
  173.3 9.2 %multiply_convert_fusion = bf16[2048,1536]{1,0:T(8,128)(2,1)} fusion(f32[2048,1536]{1,0:T(8,128)} %convert_reduce_fusion), kind=kLoop, calls=%fused_computation.4 | loop fusion | flops 6291456 | bytes 18874368 | tf_op jit(solution)/shard_map/convert_element_type | solution.py:74
  182.4 0.0 copy-start.2
  182.4 0.0 copy-start.3
  182.4 9.3 %multiply_convert_fusion.1 = bf16[1536,2048]{1,0:T(8,128)(2,1)} fusion(f32[1536,2048]{1,0:T(8,128)} %convert_reduce_fusion.1), kind=kLoop, calls=%fused_computation.5 | loop fusion | flops 6291456 | bytes 18874368 | tf_op jit(solution)/shard_map/convert_element_type | solution.py:73
  191.7 4.7 %reduce-scatter.2.cloned.1.call-done = f32[16,6144]{1,0:T(8,128)} async-done(((f32[128,6144]{1,0:T(8,128)}), f32[16,6144]{1,0:T(8,128)}) %reduce-scatter.2.cloned.1.call-update) | async-done | bytes 393232 | tf_op jit(solution)/shard_map/reduce_scatter | solution.py:35
  196.5 0.0 copy-done.2
  196.5 0.0 copy-done.3
  196.5 1.3 fusion.18
  197.8 44.4 %psum.7 = f32[6144]{0:T(1024)S(1)} all-reduce(f32[6144]{0:T(1024)S(1)} %get-tuple-element.4), channel_id=1, replica_groups=mesh['dp'=4,'mp'=8] {'dp','mp'}, use_global_device_ids=true, to_apply=%region_8.0 | all-reduce | flops 6144 | bytes 49152 | tf_op jit(solution)/shard_map/psum | solution.py:46
  242.2 0.6 broadcast_multiply_fusion
  242.8 1.8 fusion.17
  (3 shorter events, 0.0 us)
Async XLA Ops:
  7.2 30.3 %all-gather.7.cloned.1.call-start = ((), (), s32[]{:S(2)}) async-start(), calls=%async_computation.4 | async-start | bytes 1769472 | tf_op jit(solution)/shard_map/all_gather | solution.py:26
  11.2 52.3 %all-gather.5.cloned.1.call-start = ((), (), s32[]{:S(2)}) async-start(), calls=%async_computation.3 | async-start | bytes 1769472 | tf_op jit(solution)/shard_map/all_gather | solution.py:27
  12.0 117.7 %all-gather.11.cloned.1.call-start = ((), (), s32[]{:S(2)}) async-start(), calls=%async_computation.7 | async-start | bytes 2621440 | tf_op jit(solution)/shard_map/all_gather | solution.py:58
  50.6 108.7 %all-gather.9.cloned.1.call-start = ((), (), s32[]{:S(2)}) async-start(), calls=%async_computation.6 | async-start | bytes 2621440 | tf_op jit(solution)/shard_map/all_gather | solution.py:59
  77.8 14.5 %copy-start = (bf16[128,6144]{1,0:T(8,128)(2,1)S(1)}, bf16[128,6144]{1,0:T(8,128)(2,1)}, u32[]{:S(2)}) copy-start(bf16[128,6144]{1,0:T(8,128)(2,1)} %all-gather.5.cloned.1.call-done) | copy-start | bytes 4718596
  77.9 118.6 %reduce-scatter.2.cloned.1.call-start = ((), (), s32[]{:S(2)}) async-start(), calls=%async_computation.5 | async-start | bytes 3538944 | tf_op jit(solution)/shard_map/reduce_scatter | solution.py:35
  92.4 8.4 %copy-start.1 = (bf16[128,6144]{1,0:T(8,128)(2,1)S(1)}, bf16[128,6144]{1,0:T(8,128)(2,1)}, u32[]{:S(2)}) copy-start(bf16[128,6144]{1,0:T(8,128)(2,1)} %all-gather.7.cloned.1.call-done) | copy-start | bytes 4718596
  96.5 29.0 %all-to-all-start.1 = ((bf16[128,4,1536]{2,0,1:T(8,128)(2,1)}), bf16[128,4,1536]{2,0,1:T(8,128)(2,1)S(1)}, u32[]{:S(2)}, u32[]{:S(2)}) async-start(bf16[128,4,1536]{2,0,1:T(8,128)(2,1)} %copy.17), calls=%async_computation.2 | async-start | bytes 3145728 | tf_op jit(solution)/shard_map/all_to_all | solution.py:55
  125.6 33.7 %all-to-all-start = ((bf16[128,4,1536]{0,2,1:T(8,128)(2,1)}), bf16[128,4,1536]{0,2,1:T(8,128)(2,1)S(1)}, u32[]{:S(2)}, u32[]{:S(2)}) async-start(bf16[128,4,1536]{0,2,1:T(8,128)(2,1)} %bitcast), calls=%async_computation.1 | async-start | bytes 3145728 | tf_op jit(solution)/shard_map/all_to_all | solution.py:54
  182.4 14.0 %copy-start.2 = (bf16[16,6144]{1,0:T(8,128)(2,1)S(1)}, bf16[16,6144]{1,0:T(8,128)(2,1)}, u32[]{:S(2)}) copy-start(bf16[16,6144]{1,0:T(8,128)(2,1)} %param.5) | copy-start | bytes 589828
  182.4 14.0 %copy-start.3 = (f32[6144]{0:T(1024)S(1)}, f32[6144]{0:T(1024)}, u32[]{:S(2)}) copy-start(f32[6144]{0:T(1024)} %param.6) | copy-start | bytes 73732
Sparse Core Ops, SparseCore 0:
  11.4 26.0 all-gather.6
  39.1 24.3 all-gather.4
  65.4 34.6 all-gather.10
  101.8 52.6 all-gather.8
  156.6 39.8 reduce-scatter.1
where the time goes:
time: 252 us; the launch traced here: 251 us
  waiting for transfers between devices  82.5 us (33%)
  matrix products  69.9 us (28%)
  blocking collectives  44.4 us (18%)
  other arithmetic  26.2 us (10%)
  between operations  13.8 us (5%)
  starting transfers between devices  8.55 us (3%)
  local copies, waits for them, and re-layouts  5.71 us (2%)
    psum x1, blocking collectives, per_device(): lax.psum(jnp.sum(norm_grad * x_hat, axis=0), ('dp', 'mp')) * factor  44.4 us
    all_gather x1, waiting for transfers between devices, per_device(): lax.all_gather(normed, 'mp', axis=0, tiled=True)  25.4 us
    all_to_all x1, waiting for transfers between devices, per_device(): lax.all_to_all(cotan_all, 'dp', split_axis=1, concat_axis=0, tiled=True)  23.3 us
    all_to_all x1, waiting for transfers between devices, per_device(): lax.all_to_all(normed_all, 'dp', split_axis=1, concat_axis=0, tiled=True)  15.4 us
    dot_general x1, matrix products, per_device(): lax.dot_general(pre_grad, up_weight, (((1,), (1,)), ((), ())), preferred_...  14.4 us
    dot_general x1, matrix products, per_device(): lax.dot_general(cotan_all, down_weight, (((1,), (1,)), ((), ())), preferr...  14.3 us
    dot_general x1, matrix products, per_device(): jnp.einsum('rtf,rtk->rfk', stacked(hidden_all), stacked(cotan_cols), pref...  14.2 us
    dot_general x1, matrix products, per_device(): jnp.einsum('rtk,rtf->rkf', stacked(normed_cols), stacked(pre_all), prefer...  14 us
  transfers between devices with their start and end apart: 7, of which 5 were waited for; matrix products, arithmetic and copies ran while one was open for 37% of the time, Pallas kernels for 0%

commit v1 on v0

--- a/solution.py
+++ b/solution.py
@@ -22,10 +22,22 @@
     inv_std = lax.rsqrt(jnp.mean(centered * centered, axis=1, keepdims=True) + 1e-06)
     x_hat = centered * inv_std
     normed = (x_hat * norm_gain).astype(jnp.bfloat16)
-    normed_all, cotan_all = (
-        lax.all_gather(normed, "mp", axis=0, tiled=True),
-        lax.all_gather(out_grad, "mp", axis=0, tiled=True),
-    )
+
+    def wait_panel(local_x):
+        local_now, parts_out = (lax.axis_size("mp"), lax.axis_index("mp"))
+        arr_out, near = (local_x, 1)
+        while near < local_now:
+            samples = []
+            for idx in range(local_now):
+                samples.append((idx, idx ^ near))
+            block_last = lax.ppermute(arr_out, "mp", samples)
+            k_now = jnp.concatenate([arr_out, block_last], 0)
+            z = jnp.concatenate([block_last, arr_out], 0)
+            arr_out = jnp.where(parts_out & near == 0, k_now, z)
+            near = 2 * near
+        return arr_out
+
+    normed_all, cotan_all = (lax.all_gather(normed, "mp", axis=0, tiled=True), wait_panel(out_grad))
     preact = jnp.dot(normed_all, up_weight, preferred_element_type=jnp.float32)
     hidden = gelu_value(preact).astype(jnp.bfloat16)
     hid_grad = lax.dot_general(

time: 252 us -> 268 us (1.063)
  waiting for transfers between devices: 82.5 us -> 94.3 us
  other arithmetic: 26.2 us -> 30.2 us
  matrix products: 69.9 us -> 73.8 us
  local copies, waits for them, and re-layouts: 5.71 us -> 2.45 us
  blocking collectives: 44.4 us -> 41.6 us
    ppermute x0 -> x3, waiting for transfers between devices: none -> 35.8 us  [wait_panel(): block_last = lax.ppermute(arr_out, 'mp', samples)]
    all_gather x1 -> x0, waiting for transfers between devices: 12.9 us -> none  [per_device(): lax.all_gather(out_grad, 'mp', axis=0, tiled=True)]
    all_to_all x1, waiting for transfers between devices: 15.4 us -> 4.09 us  [per_device(): lax.all_to_all(normed_all, 'dp', split_axis=1, concat_axis=0, tiled=True)]
    all_to_all x1, waiting for transfers between devices: 23.3 us -> 28.6 us  [per_device(): lax.all_to_all(cotan_all, 'dp', split_axis=1, concat_axis=0, tiled=True)]
    reduce_scatter x1, waiting for transfers between devices: 4.71 us -> 0.01 us  [per_device(): lax.psum_scatter(lax.dot_general(pre_grad, up_weight, (((1,), (1,)), ((),...]
    select_n x0 -> x5, other arithmetic: none -> 4.13 us  [wait_panel(): arr_out = jnp.where(parts_out & near == 0, k_now, z)]
    dot_general x1, matrix products: 14.3 us -> 17.8 us  [per_device(): lax.dot_general(cotan_all, down_weight, (((1,), (1,)), ((), ())), preferr...]
    psum x1, blocking collectives: 44.4 us -> 41.6 us  [per_device(): lax.psum(jnp.sum(norm_grad * x_hat, axis=0), ('dp', 'mp')) * factor]
  transfers between devices with their start and end apart: 7 -> 9, of which waited for: 5 -> 5; matrix products, arithmetic and copies ran while one was open for 37% -> 37% of each run, Pallas kernels for 0% -> 0%
where the time goes in v1:
time: 268 us; the launch traced here: 267 us
  waiting for transfers between devices  94.3 us (35%)
  matrix products  73.8 us (28%)
  blocking collectives  41.6 us (16%)
  other arithmetic  30.2 us (11%)
  between operations  13.9 us (5%)
  starting transfers between devices  11.1 us (4%)
    psum x1, blocking collectives, per_device(): lax.psum(jnp.sum(norm_grad * x_hat, axis=0), ('dp', 'mp')) * factor  41.6 us
    ppermute x3, waiting for transfers between devices, wait_panel(): block_last = lax.ppermute(arr_out, 'mp', samples)  35.8 us
    all_to_all x1, waiting for transfers between devices, per_device(): lax.all_to_all(cotan_all, 'dp', split_axis=1, concat_axis=0, tiled=True)  28.6 us
    all_gather x1, waiting for transfers between devices, per_device(): lax.all_gather(normed, 'mp', axis=0, tiled=True)  25.6 us
    dot_general x1, matrix products, per_device(): lax.dot_general(cotan_all, down_weight, (((1,), (1,)), ((), ())), preferr...  17.8 us
    dot_general x1, matrix products, per_device(): lax.dot_general(pre_grad, up_weight, (((1,), (1,)), ((), ())), preferred_...  14.9 us
    dot_general x1, matrix products, per_device(): jnp.einsum('rtf,rtk->rfk', stacked(hidden_all), stacked(cotan_cols), pref...  14.2 us
    dot_general x1, matrix products, per_device(): jnp.einsum('rtk,rtf->rkf', stacked(normed_cols), stacked(pre_all), prefer...  14 us
  transfers between devices with their start and end apart: 9, of which 5 were waited for; matrix products, arithmetic and copies ran while one was open for 37% of the time, Pallas kernels for 0%

profile of v1, /device:TPU:10, one launch (start us, length us, event | category | flops | bytes accessed | tf_op | source)
XLA Modules:
  0.0 267.3 jit_solution(12098505955193288882)
XLA Ops:
  7.2 0.0 all-gather.4.cloned.1.call-start
  7.2 1.1 convert_reduce_fusion.2
  8.3 1.2 fusion.25
  9.5 1.7 fusion.19
  11.2 0.0 all-gather.4.cloned.1.call-update
  11.2 0.0 all-gather.8.cloned.1.call-start
  11.3 0.1 collective-permute-start
  11.4 1.6 collective-permute-done
  13.0 1.1 maximum_select_fusion.5
  14.1 0.5 collective-permute-start.1
  14.6 25.6 %all-gather.4.cloned.1.call-done = bf16[128,6144]{1,0:T(8,128)(2,1)} async-done(((bf16[16,6144]{1,0:T(8,128)(2,1)}), bf16[128,6144]{1,0:T(8,128)(2,1)}) %all-gather.4.cloned.1.call-update) | async-done | bytes 1572880 | tf_op jit(solution)/shard_map/all_gather | solution.py:40
  40.3 13.0 %multiply_convert_fusion.2 = (bf16[128,2048]{1,0:T(8,128)(2,1)}, f32[128,2048]{1,0:T(8,128)S(1)}) fusion(bf16[128,6144]{1,0:T(8,128)(2,1)} %all-gather.4.cloned.1.call-done, bf16[6144,2048]{1,0:T(8,128)(2,1)} %param.7), kind=kOutput, calls=%fused_computation.23 | convolution fusion | flops 3222536192 | bytes 28311552 | tf_op jit(solution)/shard_map/dot_general | solution.py:41
  53.2 0.0 all-gather.8.cloned.1.call-update
  53.3 0.0 all-gather.6.cloned.1.call-start
  53.3 0.0 collective-permute-done.1
  53.3 1.0 maximum_select_fusion.3
  54.3 1.8 collective-permute-start.2
  56.2 34.2 %collective-permute-done.2 = bf16[64,6144]{1,0:T(8,128)(2,1)S(1)} collective-permute-done((bf16[64,6144]{1,0:T(8,128)(2,1)}, bf16[64,6144]{1,0:T(8,128)(2,1)S(1)}, u32[]{:S(2)}, u32[]{:S(2)}) %collective-permute-start.2) | collective-permute-done | bytes 786464 | tf_op jit(solution)/shard_map/ppermute | solution.py:33
  90.4 0.0 copy-start.3
  90.4 17.8 %fusion = bf16[128,2048]{1,0:T(8,128)(2,1)} fusion(bf16[2048,6144]{1,0:T(8,128)(2,1)} %param.8, bf16[64,6144]{1,0:T(8,128)(2,1)S(1)} %collective-permute-done.2, bf16[64,6144]{1,0:T(8,128)(2,1)} %maximum_select_fusion.3, pred[]{:T(512)S(6)} %eq.9, f32[128,2048]{1,0:T(8,128)S(1)} %get-tuple-element.8), kind=kOutput, calls=%fused_computation.7 | convolution fusion | flops 3230924800 | bytes 28311552 | tf_op jit(solution)/shard_map/dot_general | solution.py:43
  108.2 0.0 all-gather.6.cloned.1.call-update
  108.2 0.0 reduce-scatter.2.cloned.1.call-start
  108.3 0.0 copy-done.3
  108.3 0.1 maximum_select_fusion.6
  108.4 0.0 copy-start.2
  108.5 0.2 maximum_select_fusion.4
  108.6 0.1 copy.31
  108.7 0.8 copy-done.2
  109.5 14.9 %fusion.27 = f32[128,6144]{1,0:T(8,128)} fusion(bf16[128,2048]{1,0:T(8,128)(2,1)S(1)} %copy-done.2, bf16[6144,2048]{1,0:T(8,128)(2,1)} %param.7), kind=kOutput, calls=%fused_computation.55 | convolution fusion | flops 3221225472 | bytes 28835840 | tf_op jit(solution)/shard_map/dot_general | solution.py:48
  124.3 0.0 reduce-scatter.2.cloned.1.call-update
  124.3 1.8 maximum_select_fusion.2
  126.1 0.0 copy-start
  126.1 4.4 %all-to-all-start.1 = ((bf16[128,4,1536]{2,0,1:T(8,128)(2,1)}), bf16[128,4,1536]{2,0,1:T(8,128)(2,1)S(1)}, u32[]{:S(2)}, u32[]{:S(2)}) async-start(bf16[128,4,1536]{2,0,1:T(8,128)(2,1)} %maximum_select_fusion.2), calls=%async_computation.2 | async-start | bytes 3145728 | tf_op jit(solution)/shard_map/all_to_all | solution.py:67
  130.5 0.0 copy-done
  130.5 1.6 copy.22
  132.1 28.6 %all-to-all-done.1 = bf16[128,4,1536]{2,0,1:T(8,128)(2,1)S(1)} async-done(((bf16[128,4,1536]{2,0,1:T(8,128)(2,1)}), bf16[128,4,1536]{2,0,1:T(8,128)(2,1)S(1)}, u32[]{:S(2)}, u32[]{:S(2)}) %all-to-all-start.1) | async-done | bytes 1572896 | tf_op jit(solution)/shard_map/all_to_all | solution.py:67
  160.7 4.1 %all-to-all-start = ((bf16[128,4,1536]{0,2,1:T(8,128)(2,1)}), bf16[128,4,1536]{0,2,1:T(8,128)(2,1)S(1)}, u32[]{:S(2)}, u32[]{:S(2)}) async-start(bf16[128,4,1536]{0,2,1:T(8,128)(2,1)} %bitcast), calls=%async_computation.1 | async-start | bytes 3145728 | tf_op jit(solution)/shard_map/all_to_all | solution.py:66
  164.8 0.0 all-gather.8.cloned.1.call-done
  164.8 14.2 %convert_reduce_fusion = f32[2048,1536]{1,0:T(8,128)} fusion(bf16[4,128,2048]{2,1,0:T(8,128)(2,1)} %bitcast.33, bf16[128,4,1536]{2,0,1:T(8,128)(2,1)S(1)} %all-to-all-done.1), kind=kOutput, calls=%fused_computation | convolution fusion | flops 3255828480 | bytes 16252928 | tf_op jit(solution)/shard_map/rtf,rtk->rfk/dot_general | solution.py:80
  179.0 4.1 %all-to-all-done = bf16[128,4,1536]{0,2,1:T(8,128)(2,1)S(1)} async-done(((bf16[128,4,1536]{0,2,1:T(8,128)(2,1)}), bf16[128,4,1536]{0,2,1:T(8,128)(2,1)S(1)}, u32[]{:S(2)}, u32[]{:S(2)}) %all-to-all-start) | async-done | bytes 1572896 | tf_op jit(solution)/shard_map/all_to_all | solution.py:66
  183.1 0.0 all-gather.6.cloned.1.call-done
  183.1 14.0 %convert_reduce_fusion.1 = f32[1536,2048]{1,0:T(8,128)} fusion(bf16[4,128,2048]{2,1,0:T(8,128)(2,1)} %bitcast.34, bf16[128,4,1536]{0,2,1:T(8,128)(2,1)S(1)} %all-to-all-done), kind=kOutput, calls=%fused_computation.1 | convolution fusion | flops 3255828480 | bytes 16252928 | tf_op jit(solution)/shard_map/rtk,rtf->rkf/dot_general | solution.py:77
  197.1 9.2 %multiply_convert_fusion.1 = bf16[1536,2048]{1,0:T(8,128)(2,1)} fusion(f32[1536,2048]{1,0:T(8,128)} %convert_reduce_fusion.1), kind=kLoop, calls=%fused_computation.5 | loop fusion | flops 6291456 | bytes 18874368 | tf_op jit(solution)/shard_map/convert_element_type | solution.py:85
  206.3 0.0 copy-start.1
  206.3 0.0 copy-start.4
  206.3 9.0 %multiply_convert_fusion = bf16[2048,1536]{1,0:T(8,128)(2,1)} fusion(f32[2048,1536]{1,0:T(8,128)} %convert_reduce_fusion), kind=kLoop, calls=%fused_computation.4 | loop fusion | flops 6291456 | bytes 18874368 | tf_op jit(solution)/shard_map/convert_element_type | solution.py:86
  215.4 0.0 reduce-scatter.2.cloned.1.call-done
  215.4 0.0 copy-done.1
  215.4 0.0 copy-done.4
  215.4 1.3 fusion.24
  216.7 41.6 %psum.7 = f32[6144]{0:T(1024)S(1)} all-reduce(f32[6144]{0:T(1024)S(1)} %get-tuple-element.4), channel_id=1, replica_groups=mesh['dp'=4,'mp'=8] {'dp','mp'}, use_global_device_ids=true, to_apply=%region_8.9 | all-reduce | flops 6144 | bytes 49152 | tf_op jit(solution)/shard_map/psum | solution.py:58
  258.3 0.6 broadcast_multiply_fusion
  258.9 1.8 fusion.23
  (6 shorter events, 0.1 us)
Async XLA Ops:
  7.2 33.1 %all-gather.4.cloned.1.call-start = ((), (), s32[]{:S(2)}) async-start(), calls=%async_computation.3 | async-start | bytes 1769472 | tf_op jit(solution)/shard_map/all_gather | solution.py:40
  11.2 153.6 %all-gather.8.cloned.1.call-start = ((), (), s32[]{:S(2)}) async-start(), calls=%async_computation.6 | async-start | bytes 2621440 | tf_op jit(solution)/shard_map/all_gather | solution.py:70
  11.3 1.7 collective-permute-start
  14.1 39.2 %collective-permute-start.1 = (bf16[32,6144]{1,0:T(8,128)(2,1)S(1)}, bf16[32,6144]{1,0:T(8,128)(2,1)S(1)}, u32[]{:S(2)}, u32[]{:S(2)}) collective-permute-start(bf16[32,6144]{1,0:T(8,128)(2,1)S(1)} %maximum_select_fusion.5), channel_id=1, source_target_pairs={{0,2},{1,3},{2,0},{3,1},{4,6},{5,7},{6,4},{7,5},{8,10},{9,11},{10,... | collective-permute-start | bytes 1179656 | tf_op jit(solution)/shard_map/ppermute | solution.py:33
  53.3 129.8 %all-gather.6.cloned.1.call-start = ((), (), s32[]{:S(2)}) async-start(), calls=%async_computation.5 | async-start | bytes 2621440 | tf_op jit(solution)/shard_map/all_gather | solution.py:71
  54.3 36.1 %collective-permute-start.2 = (bf16[64,6144]{1,0:T(8,128)(2,1)}, bf16[64,6144]{1,0:T(8,128)(2,1)S(1)}, u32[]{:S(2)}, u32[]{:S(2)}) collective-permute-start(bf16[64,6144]{1,0:T(8,128)(2,1)} %maximum_select_fusion.3), channel_id=1, source_target_pairs={{0,4},{1,5},{2,6},{3,7},{4,0},{5,1},{6,2},{7,3},{8,12},{9,13},{10,... | collective-permute-start | bytes 2359304 | tf_op jit(solution)/shard_map/ppermute | solution.py:33
  90.4 17.9 %copy-start.3 = (bf16[16,6144]{1,0:T(8,128)(2,1)S(1)}, bf16[16,6144]{1,0:T(8,128)(2,1)}, u32[]{:S(2)}) copy-start(bf16[16,6144]{1,0:T(8,128)(2,1)} %param.9) | copy-start | bytes 589828
  108.2 107.1 %reduce-scatter.2.cloned.1.call-start = ((), (), s32[]{:S(2)}) async-start(), calls=%async_computation.4 | async-start | bytes 3538944 | tf_op jit(solution)/shard_map/reduce_scatter | solution.py:47
  108.4 1.0 copy-start.2
  126.1 4.4 %copy-start = (bf16[128,6144]{1,0:T(8,128)(2,1)S(1)}, bf16[128,6144]{1,0:T(8,128)(2,1)}, u32[]{:S(2)}) copy-start(bf16[128,6144]{1,0:T(8,128)(2,1)} %all-gather.4.cloned.1.call-done) | copy-start | bytes 4718596
  126.1 34.6 %all-to-all-start.1 = ((bf16[128,4,1536]{2,0,1:T(8,128)(2,1)}), bf16[128,4,1536]{2,0,1:T(8,128)(2,1)S(1)}, u32[]{:S(2)}, u32[]{:S(2)}) async-start(bf16[128,4,1536]{2,0,1:T(8,128)(2,1)} %maximum_select_fusion.2), calls=%async_computation.2 | async-start | bytes 3145728 | tf_op jit(solution)/shard_map/all_to_all | solution.py:67
  160.7 22.4 %all-to-all-start = ((bf16[128,4,1536]{0,2,1:T(8,128)(2,1)}), bf16[128,4,1536]{0,2,1:T(8,128)(2,1)S(1)}, u32[]{:S(2)}, u32[]{:S(2)}) async-start(bf16[128,4,1536]{0,2,1:T(8,128)(2,1)} %bitcast), calls=%async_computation.1 | async-start | bytes 3145728 | tf_op jit(solution)/shard_map/all_to_all | solution.py:66
  206.3 9.1 %copy-start.1 = (bf16[16,6144]{1,0:T(8,128)(2,1)S(1)}, bf16[16,6144]{1,0:T(8,128)(2,1)}, u32[]{:S(2)}) copy-start(bf16[16,6144]{1,0:T(8,128)(2,1)} %param.5) | copy-start | bytes 589828
  206.3 9.1 %copy-start.4 = (f32[6144]{0:T(1024)S(1)}, f32[6144]{0:T(1024)}, u32[]{:S(2)}) copy-start(f32[6144]{0:T(1024)} %param.6) | copy-start | bytes 73732
Sparse Core Ops, SparseCore 0:
  11.4 28.8 all-gather.3
  53.4 35.5 all-gather.7
  108.4 48.3 all-gather.5
  158.9 41.2 reduce-scatter.1
